TPU v7x, 32 devices: a whole 2x2x4 slice. The times are simulated.
32 devices in a mesh: mem: 16 (over z, y, core), lat: 2 (over x).
Axes of the slice: x: 2, y: 2, z: 4, core: 2. Of those that a mesh axis runs over, the one named last changes fastest.
Arguments:
- controls: bfloat16 [64, 64, 256, 256], P('mem', None, 'lat'), may hold values from -6 to 6
- spread: bfloat16 [64, 64, 256, 256], P('mem', None, 'lat'), may hold values from -1.5 to 1.5
- classes: int32 [256, 256], P('lat'), may hold values from 0 to 7
- prec_table: float32 [8, 64], replicated, may hold values from 0.25 to 4
- vert_loc: bfloat16 [64, 64], replicated, may hold values from 0 to 1
- lon_loc: bfloat16 [256, 256], replicated, may hold values from 0 to 1
- lat_loc: bfloat16 [256, 256], replicated, may hold values from 0 to 1
Outputs:
- localized: bfloat16 [64, 64, 256, 256], P('mem', None, 'lat')
All inputs are finite; a program needn't handle non-finite values.
Results may differ from a plain program's by a relative error of at most 0.0064.
Values may be sent and summed in bfloat16 or wider, within the bound.
A program may use at most 128 MiB of HBM per device.

v0:
```python
import jax
import jax.numpy as jnp
from jax import lax
from jax.sharding import PartitionSpec as P


def lookup(table, classes):
    numbers = jnp.arange(table.shape[0], dtype=jnp.int32)
    onehot = (classes[None, :, :] == numbers[:, None, None]).astype(jnp.float32)
    return jnp.einsum("kl,kab->lab", table, onehot, precision=lax.Precision.HIGHEST)


def local(controls, spread, classes, prec_table, vert_loc, lon_loc, lat_loc):
    partial_value = jnp.sum(spread.astype(jnp.float32) * controls.astype(jnp.float32), axis=0)
    shares = lax.psum_scatter(partial_value, "mem", scatter_dimension=0, tiled=True)
    level_count = shares.shape[0]
    table_rows = lax.dynamic_slice_in_dim(
        prec_table, lax.axis_index("mem") * level_count, level_count, 1
    )
    weighted_part = shares * lookup(table_rows, classes)
    weighted = lax.all_gather(weighted_part, "mem", axis=0, tiled=True)
    adjoint = (spread.astype(jnp.float32) * weighted[None]).astype(jnp.bfloat16)
    along_lon = jnp.einsum(
        "mlac,bc->mlab", adjoint, lon_loc, preferred_element_type=jnp.float32
    ).astype(jnp.bfloat16)
    sending = jnp.einsum(
        "lj,mjab->mlab", vert_loc, along_lon, preferred_element_type=jnp.float32
    ).astype(jnp.bfloat16)
    return jnp.einsum(
        "ac,mlcb->mlba",
        lat_loc,
        lax.all_to_all(sending, "lat", split_axis=3, concat_axis=2, tiled=True),
        preferred_element_type=jnp.float32,
    ).astype(jnp.bfloat16)


def solution(mesh):
    return jax.shard_map(
        local,
        mesh=mesh,
        in_specs=(
            P("mem", None, "lat", None),
            P("mem", None, "lat", None),
            P("lat", None),
            P(),
            P(),
            P(),
            P(),
        ),
        out_specs=P("mem", None, "lat", None),
        check_vma=False,
    )
```

profile of v0, /device:TPU:0, one launch (start us, length us, event | category | flops | bytes accessed | tf_op | source)
XLA Modules:
  0.0 539.2 jit_solution(17640405347638670509)
XLA Ops:
  6.5 0.0 copy-start
  6.5 0.0 copy-start.5
  6.5 0.0 copy-start.3
  6.5 0.0 reduce-scatter.2.cloned.1.call-start
  6.5 17.7 %fusion = f32[64,128,256]{2,1,0:T(8,128)} fusion(bf16[4,64,128,256]{3,2,1,0:T(8,128)(2,1)} %param.8, bf16[4,64,128,256]{3,2,1,0:T(8,128)(2,1)} %param.7), kind=kLoop, calls=%fused_computation.2 | loop fusion | flops 31457280 | bytes 41943040 | tf_op jit(solution)/shard_map/reduce_sum | solution.py:14
  24.3 0.0 reduce-scatter.2.cloned.1.call-update
  24.3 0.0 all-gather.2.cloned.1.call-start
  24.3 0.0 copy-done.5
  24.3 0.0 copy-done.3
  24.4 0.7 fusion.14
  25.1 105.5 %reduce-scatter.2.cloned.1.call-done = f32[4,128,256]{2,1,0:T(8,128)} async-done(((f32[64,128,256]{2,1,0:T(8,128)}), f32[4,128,256]{2,1,0:T(8,128)}) %reduce-scatter.2.cloned.1.call-update) | async-done | bytes 524304 | tf_op jit(solution)/shard_map/reduce_scatter | solution.py:15
  130.6 2.0 copy_multiply_fusion
  132.6 0.0 all-gather.2.cloned.1.call-update
  132.6 0.0 copy-start.4
  132.6 74.1 %all-gather.2.cloned.1.call-done = f32[64,128,256]{2,1,0:T(8,128)} async-done(((f32[4,128,256]{2,1,0:T(8,128)}), f32[64,128,256]{2,1,0:T(8,128)}) %all-gather.2.cloned.1.call-update) | async-done | bytes 8388624 | tf_op jit(solution)/shard_map/all_gather | solution.py:21
  206.7 16.6 %fusion.1 = bf16[4,64,128,256]{3,2,1,0:T(8,128)(2,1)} fusion(bf16[4,64,128,256]{3,2,1,0:T(8,128)(2,1)} %param.8, f32[64,128,256]{2,1,0:T(8,128)} %all-gather.2.cloned.1.call-done), kind=kLoop, calls=%fused_computation.3 | loop fusion | flops 25165824 | bytes 41943040 | tf_op jit(solution)/shard_map/convert_element_type | solution.py:22
  223.4 0.0 copy-done
  223.4 0.0 copy-done.4
  223.4 19.1 %convert_bitcast_fusion = bf16[4,64,128,256]{3,1,2,0:T(8,128)(2,1)} fusion(bf16[4,64,128,256]{3,2,1,0:T(8,128)(2,1)} %fusion.1, bf16[256,256]{1,0:T(8,128)(2,1)S(1)} %copy-done, bf16[64,64]{1,0:T(8,128)(2,1)S(1)} %copy-done.4), kind=kOutput, calls=%fused_computation.7 | convolution fusion | flops 5385486336 | bytes 33693696 | tf_op jit(solution)/shard_map/lj,mjab->mlab/dot_general | solution.py:26
  242.5 25.8 %copy.25 = bf16[4,64,128,256]{2,1,0,3:T(8,128)(2,1)} copy(bf16[4,64,128,256]{3,1,2,0:T(8,128)(2,1)} %convert_bitcast_fusion) | data formatting | bytes 33554432 | tf_op jit(solution)/shard_map/convert_element_type | solution.py:28
  268.3 188.7 %all_to_all.18 = bf16[4,64,128,256]{2,1,0,3:T(8,128)(2,1)S(1)} all-to-all(bf16[4,64,128,256]{2,1,0,3:T(8,128)(2,1)} %copy.25), channel_id=1, replica_groups=mesh['mem'=16,'lat'=2] {'lat'}, dimensions={3} | all-to-all | bytes 33554432 | tf_op jit(solution)/shard_map/all_to_all | solution.py:32
  457.0 36.5 %copy.41 = bf16[4,64,128,2,128]{2,3,4,1,0:T(2,128)(2,1)} copy(bf16[4,64,128,2,128]{2,1,0,4,3:T(8,128)(2,1)S(1)} %bitcast.29) | data formatting | bytes 33554432 | tf_op jit(solution)/shard_map/all_to_all | solution.py:32
  493.5 0.0 copy-start.2
  493.5 0.0 copy-start.1
  493.5 27.0 %all_to_all.16 = bf16[4,64,256,128]{2,3,1,0:T(8,128)(2,1)} reshape(bf16[4,64,2,128,128]{3,2,4,1,0:T(2,128)(2,1)} %bitcast.30) | data formatting | bytes 33554432 | tf_op jit(solution)/shard_map/all_to_all | solution.py:32
  520.4 0.0 copy-done.2
  520.4 11.9 %convolution_convert_fusion = bf16[4,64,128,256]{3,2,1,0:T(8,128)(2,1)} fusion(bf16[4,64,256,128]{2,3,1,0:T(8,128)(2,1)} %all_to_all.16, bf16[256,256]{1,0:T(8,128)(2,1)S(1)} %copy-done.2), kind=kOutput, calls=%fused_computation.10 | convolution fusion | flops 4303355904 | bytes 33685504 | tf_op jit(solution)/shard_map/ac,mlcb->mlba/dot_general | solution.py:29
  532.4 0.0 copy-done.1
Async XLA Ops:
  6.5 216.8 %copy-start = (bf16[256,256]{1,0:T(8,128)(2,1)S(1)}, bf16[256,256]{1,0:T(8,128)(2,1)}, u32[]{:S(2)}) copy-start(bf16[256,256]{1,0:T(8,128)(2,1)} %param.12) | copy-start | bytes 393220
  6.5 17.8 %copy-start.5 = (f32[8,64]{1,0:T(8,128)S(1)}, f32[8,64]{1,0:T(8,128)}, u32[]{:S(2)}) copy-start(f32[8,64]{1,0:T(8,128)} %param.10) | copy-start | bytes 6148
  6.5 17.8 %copy-start.3 = (s32[128,256]{1,0:T(8,128)S(1)}, s32[128,256]{1,0:T(8,128)}, u32[]{:S(2)}) copy-start(s32[128,256]{1,0:T(8,128)} %param.9) | copy-start | bytes 393220
  6.5 124.1 %reduce-scatter.2.cloned.1.call-start = ((), (), s32[]{:S(2)}) async-start(), calls=%async_computation.2 | async-start | bytes 8912896 | tf_op jit(solution)/shard_map/reduce_scatter | solution.py:15
  24.3 182.5 %all-gather.2.cloned.1.call-start = ((), (), s32[]{:S(2)}) async-start(), calls=%async_computation.3 | async-start | bytes 8912896 | tf_op jit(solution)/shard_map/all_gather | solution.py:21
  132.6 90.8 %copy-start.4 = (bf16[64,64]{1,0:T(8,128)(2,1)S(1)}, bf16[64,64]{1,0:T(8,128)(2,1)}, u32[]{:S(2)}) copy-start(bf16[64,64]{1,0:T(8,128)(2,1)} %param.11) | copy-start | bytes 24580
  493.5 27.0 %copy-start.2 = (bf16[256,256]{1,0:T(8,128)(2,1)S(1)}, bf16[256,256]{1,0:T(8,128)(2,1)}, u32[]{:S(2)}) copy-start(bf16[256,256]{1,0:T(8,128)(2,1)} %param.13) | copy-start | bytes 393220
  493.5 38.9 %copy-start.1 = (bf16[256,256]{1,0:T(8,128)(2,1)S(1)}, bf16[256,256]{1,0:T(8,128)(2,1)}, u32[]{:S(2)}) copy-start(bf16[256,256]{1,0:T(8,128)(2,1)} %param.12) | copy-start | bytes 393220
Sparse Core Ops, SparseCore 0:
  24.4 106.1 reduce-scatter.1
  132.8 73.9 all-gather.1
where the time goes:
time: 541 us; the launch traced here: 539 us
  blocking collectives  189 us (35%)
  waiting for transfers between devices  180 us (33%)
  local copies, waits for them, and re-layouts  89.2 us (16%)
  other arithmetic  36.3 us (7%)
  matrix products  31.8 us (6%)
  between operations  13.4 us (2%)
    all_to_all x1, blocking collectives, local(): lax.all_to_all(sending, 'lat', split_axis=3, concat_axis=2, tiled=True)  189 us
    reduce_scatter x1, waiting for transfers between devices, local(): lax.psum_scatter(partial_value, 'mem', scatter_dimension=0, tiled=True)  106 us
    all_gather x1, waiting for transfers between devices, local(): weighted = lax.all_gather(weighted_part, 'mem', axis=0, tiled=True)  74.1 us
    all_to_all x2, local copies, waits for them, and re-layouts, local(): lax.all_to_all(sending, 'lat', split_axis=3, concat_axis=2, tiled=True)  63.4 us
    convert_element_type x1, local copies, waits for them, and re-layouts, local(): sending = jnp.einsum('lj,mjab->mlab', vert_loc, along_lon, preferred_elem...  25.8 us
    dot_general x1, matrix products, local(): jnp.einsum('lj,mjab->mlab', vert_loc, along_lon, preferred_element_type=j...  19.1 us
    reduce_sum x1, other arithmetic, local(): jnp.sum(spread.astype(jnp.float32) * controls.astype(jnp.float32), axis=0)  17.7 us
    convert_element_type x1, other arithmetic, local(): adjoint = (spread.astype(jnp.float32) * weighted[None]).astype(jnp.bfloat16)  16.6 us
  transfers between devices with their start and end apart: 2, of which 2 were waited for; matrix products, arithmetic and copies ran while one was open for 0% of the time, Pallas kernels for 0%

commit v1 on v0

v1 whole, which is shorter than its diff:
```python
import functools

import jax
import jax.numpy as jnp
from jax import lax
from jax.experimental import pallas as pl
from jax.experimental.pallas import tpu as pltpu
from jax.sharding import PartitionSpec as P

CHUNKS = 4
MIN_ROWS = 16
LANES = 128


def lookup(table, classes):
    numbers = jnp.arange(table.shape[0], dtype=jnp.int32)
    onehot = (classes[None, :, :] == numbers[:, None, None]).astype(jnp.float32)
    return jnp.einsum("kl,kab->lab", table, onehot, precision=lax.Precision.HIGHEST)


def last_kernel(count, *refs):
    pieces, weights_ref, out_ref = refs[:count], refs[count], refs[count + 1]
    weights = weights_ref[...]
    for level in range(out_ref.shape[1]):
        rows = jnp.concatenate([piece[0, level] for piece in pieces], axis=0)
        out_ref[0, level] = jnp.dot(
            rows.T, weights, preferred_element_type=jnp.float32
        ).astype(out_ref.dtype)


def along_lat(pieces, weights, levels_per_step=8):
    members, levels, _, width = pieces[0].shape
    step = min(levels_per_step, levels)
    total = weights.shape[1]
    in_specs = [
        pl.BlockSpec((1, step, piece.shape[2], width), lambda m, l: (m, l, 0, 0))
        for piece in pieces
    ] + [pl.BlockSpec(weights.shape, lambda m, l: (0, 0))]
    return pl.pallas_call(
        functools.partial(last_kernel, len(pieces)),
        grid=(members, levels // step),
        out_shape=jax.ShapeDtypeStruct((members, levels, width, total), jnp.bfloat16),
        in_specs=in_specs,
        out_specs=pl.BlockSpec((1, step, width, total), lambda m, l: (m, l, 0, 0)),
        compiler_params=pltpu.CompilerParams(
            dimension_semantics=("arbitrary", "arbitrary")
        ),
    )(*pieces, weights)


def sum_kernel(spread_ref, controls_ref, out_ref):
    total = spread_ref[0].astype(jnp.float32) * controls_ref[0].astype(jnp.float32)
    for member in range(1, spread_ref.shape[0]):
        total += spread_ref[member].astype(jnp.float32) * controls_ref[member].astype(jnp.float32)
    out_ref[...] = total


def member_sum(spread, controls, chunk, rows, levels_per_step=16):
    members, levels, _, cols = spread.shape
    step = min(levels_per_step, levels)
    block = pl.BlockSpec((members, step, rows, cols), lambda l: (0, l, chunk, 0))
    size = members * levels * rows * cols
    return pl.pallas_call(
        sum_kernel,
        grid=(levels // step,),
        out_shape=jax.ShapeDtypeStruct((levels, rows, cols), jnp.float32),
        in_specs=[block, block],
        out_specs=pl.BlockSpec((step, rows, cols), lambda l: (l, 0, 0)),
        cost_estimate=pl.CostEstimate(flops=2 * size, bytes_accessed=5 * size, transcendentals=0),
        compiler_params=pltpu.CompilerParams(dimension_semantics=("arbitrary",)),
    )(spread, controls)


def middle_kernel(width, spread_ref, weighted_ref, lon_ref, vert_ref, *refs):
    total = lon_ref.shape[1]
    pieces, groups = total // width, total // LANES
    out_refs = refs[:pieces]
    before, after = refs[pieces : pieces + groups], refs[pieces + groups :]
    _, levels, rows, cols = spread_ref.shape
    adjoint = (
        spread_ref[0].astype(jnp.float32) * weighted_ref[...].astype(jnp.float32)
    ).astype(jnp.bfloat16)
    along_lon = (
        jnp.dot(
            adjoint.reshape(levels * rows, cols), lon_ref[...], preferred_element_type=jnp.float32
        )
        .astype(jnp.bfloat16)
        .astype(jnp.float32)
    )
    for g in range(groups):
        before[g][...] = along_lon[:, g * LANES : (g + 1) * LANES]
    vert = vert_ref[...]
    for row in range(rows):
        strided = pl.ds(row, levels, stride=rows)
        column = jnp.concatenate([half[strided, :] for half in before], axis=1)
        along_lev = jnp.dot(
            vert, column.astype(jnp.bfloat16), preferred_element_type=jnp.float32
        )
        for g in range(groups):
            after[g][strided, :] = along_lev[:, g * LANES : (g + 1) * LANES]
    joined = jnp.concatenate([half[...] for half in after], axis=1).astype(jnp.bfloat16)
    for s, out_ref in enumerate(out_refs):
        out_ref[0] = joined[:, s * width : (s + 1) * width].reshape(levels, rows, width)


def lon_and_lev(spread, weighted, lon_columns, vert_loc, chunk, rows, width):
    members, levels, _, cols = spread.shape
    total = lon_columns.shape[1]
    pieces = total // width
    size = members * levels * rows * cols
    return pl.pallas_call(
        functools.partial(middle_kernel, width),
        grid=(members,),
        out_shape=[jax.ShapeDtypeStruct((members, levels, rows, width), jnp.bfloat16)] * pieces,
        in_specs=[
            pl.BlockSpec((1, levels, rows, cols), lambda m: (m, 0, chunk, 0)),
            pl.BlockSpec(weighted.shape, lambda m: (0, 0, 0)),
            pl.BlockSpec(lon_columns.shape, lambda m: (0, 0)),
            pl.BlockSpec(vert_loc.shape, lambda m: (0, 0)),
        ],
        out_specs=[pl.BlockSpec((1, levels, rows, width), lambda m: (m, 0, 0, 0))] * pieces,
        scratch_shapes=[pltpu.VMEM((levels * rows, LANES), jnp.float32)] * (2 * total // LANES),
        cost_estimate=pl.CostEstimate(
            flops=2 * size * (cols + levels), bytes_accessed=4 * size, transcendentals=0
        ),
        compiler_params=pltpu.CompilerParams(dimension_semantics=("arbitrary",)),
    )(spread, weighted, lon_columns, vert_loc)


def local(mem_count, lat_count, controls, spread, classes, prec_table, vert_loc, lon_loc, lat_loc):
    levels, rows = controls.shape[1:3]
    width = lon_loc.shape[0] // lat_count
    here, member_at = lax.axis_index("lat"), lax.axis_index("mem")
    chunk_rows = max(min(MIN_ROWS, rows), rows // CHUNKS)
    chunks = rows // chunk_rows
    lon_all = jnp.concatenate(
        [
            lax.dynamic_slice_in_dim(lon_loc, lax.rem(here + s, lat_count) * width, width, 0)
            for s in range(lat_count)
        ],
        axis=0,
    ).T
    strides, stride = [], 1
    while stride < mem_count:
        strides.append(stride)
        stride *= 2
    bits = [lax.rem(lax.div(member_at, stride), 2) for stride in strides]

    def swap(value, stride):
        return lax.ppermute(value, "mem", [(i, i ^ stride) for i in range(mem_count)])

    first, size = 0, levels
    for bit in bits:
        size //= 2
        first = first + bit * size
    table_rows = lax.dynamic_slice_in_dim(prec_table, first, size, 1)

    def weighted_of(k):
        total = member_sum(spread, controls, k, chunk_rows)
        for bit, stride in zip(bits, strides):
            half = total.shape[0] // 2
            keep = lax.dynamic_slice_in_dim(total, bit * half, half, 0)
            away = lax.dynamic_slice_in_dim(total, (1 - bit) * half, half, 0)
            total = keep + swap(away.astype(jnp.bfloat16), stride).astype(jnp.float32)
        part = classes[k * chunk_rows : (k + 1) * chunk_rows]
        value = (total * lookup(table_rows, part)).astype(jnp.bfloat16)
        for bit, stride in reversed(list(zip(bits, strides))):
            other = swap(value, stride)
            value = jnp.where(
                bit == 0,
                jnp.concatenate([value, other], axis=0),
                jnp.concatenate([other, value], axis=0),
            )
        return value

    got = [[] for _ in range(lat_count)]
    for k in range(chunks):
        blocks = lon_and_lev(spread, weighted_of(k), lon_all, vert_loc, k, chunk_rows, width)
        for s in range(lat_count):
            block = blocks[s]
            if s:
                block = lax.ppermute(
                    block, "lat", [(i, (i + s) % lat_count) for i in range(lat_count)]
                )
            got[s].append(block)
    lat_columns = jnp.concatenate(
        [
            lax.dynamic_slice_in_dim(
                lat_loc, lax.rem(here + lat_count - s, lat_count) * rows, rows, 1
            )
            for s in range(lat_count)
        ],
        axis=1,
    )
    return along_lat([piece for group in got for piece in group], lat_columns.T)


def solution(mesh):
    return jax.shard_map(
        functools.partial(local, mesh.shape["mem"], mesh.shape["lat"]),
        mesh=mesh,
        in_specs=(
            P("mem", None, "lat", None),
            P("mem", None, "lat", None),
            P("lat", None),
            P(),
            P(),
            P(),
            P(),
        ),
        out_specs=P("mem", None, "lat", None),
        check_vma=False,
    )
```

time: 541 us -> 356 us (0.66)
  blocking collectives: 189 us -> 0 us
  Pallas kernels: 0 us -> 122 us
  local copies, waits for them, and re-layouts: 89.2 us -> 10.8 us
  starting transfers between devices: 0.04 us -> 39.9 us
  matrix products: 31.8 us -> 3.08 us
  waiting for transfers between devices: 180 us -> 159 us
  other arithmetic: 36.3 us -> 18.2 us
  between operations: 13.4 us -> 0.72 us
    all_to_all x1 -> x0, blocking collectives: 189 us -> none  [local(): lax.all_to_all(sending, 'lat', split_axis=3, concat_axis=2, tiled=True)]
    ppermute x0 -> x36, waiting for transfers between devices: none -> 159 us  [the longest x4 117 us: local(): lax.ppermute(block, 'lat', [(i, (i + s) % lat_count) for i in range(lat_c...]
    pallas_call x0 -> x9, Pallas kernels: none -> 122 us  [the longest x4 71.8 us: lon_and_lev(): pl.pallas_call(functools.partial(middle_kernel, width), grid=(members,),...]
    reduce_scatter x1 -> x0, waiting for transfers between devices: 106 us -> none  [local(): lax.psum_scatter(partial_value, 'mem', scatter_dimension=0, tiled=True)]
    all_gather x1 -> x0, waiting for transfers between devices: 74.1 us -> none  [local(): weighted = lax.all_gather(weighted_part, 'mem', axis=0, tiled=True)]
    all_to_all x2 -> x0, local copies, waits for them, and re-layouts: 63.4 us -> none  [local(): lax.all_to_all(sending, 'lat', split_axis=3, concat_axis=2, tiled=True)]
    ppermute x0 -> x36, starting transfers between devices: none -> 39.9 us  [the longest x32 35.8 us: swap(): lax.ppermute(value, 'mem', [(i, i ^ stride) for i in range(mem_count)])]
    dot_general x2 -> x0, matrix products: 31.1 us -> none  [the longest x1 19.1 us: local(): jnp.einsum('lj,mjab->mlab', vert_loc, along_lon, preferred_element_type=j...]
  transfers between devices with their start and end apart: 2 -> 36, of which waited for: 2 -> 16; matrix products, arithmetic and copies ran while one was open for 0% -> 8% of each run, Pallas kernels for 0% -> 25%
where the time goes in v1:
time: 356 us; the launch traced here: 354 us
  waiting for transfers between devices  159 us (45%)
  Pallas kernels  122 us (34%)
  starting transfers between devices  39.9 us (11%)
  other arithmetic  18.2 us (5%)
  local copies, waits for them, and re-layouts  10.8 us (3%)
    ppermute x4, waiting for transfers between devices, local(): lax.ppermute(block, 'lat', [(i, (i + s) % lat_count) for i in range(lat_c...  117 us
    pallas_call x4, Pallas kernels, lon_and_lev(): pl.pallas_call(functools.partial(middle_kernel, width), grid=(members,),...  71.8 us
    ppermute x32, waiting for transfers between devices, swap(): lax.ppermute(value, 'mem', [(i, i ^ stride) for i in range(mem_count)])  41.7 us
    ppermute x32, starting transfers between devices, swap(): lax.ppermute(value, 'mem', [(i, i ^ stride) for i in range(mem_count)])  35.8 us
    pallas_call x1, Pallas kernels, along_lat(): pl.pallas_call(functools.partial(last_kernel, len(pieces)), grid=(members...  26.7 us
    pallas_call x4, Pallas kernels, member_sum(): pl.pallas_call(sum_kernel, grid=(levels // step,), out_shape=jax.ShapeDty...  23.7 us
    select_n x16, other arithmetic, weighted_of(): jnp.where(bit == 0, jnp.concatenate([value, other], axis=0), jnp.concaten...  10.9 us
  transfers between devices with their start and end apart: 36, of which 16 were waited for; matrix products, arithmetic and copies ran while one was open for 8% of the time, Pallas kernels for 25%

profile of v1, /device:TPU:0, one launch (start us, length us, event | category | flops | bytes accessed | tf_op | source)
XLA Modules:
  0.0 353.5 jit_solution(9092715870772197839)
XLA Ops:
  0.0 5.9 %shard_map.75 = f32[64,32,256]{2,1,0:T(8,128)} custom-call(bf16[4,64,128,256]{3,2,1,0:T(8,128)(2,1)} %spread_ref.15, bf16[4,64,128,256]{3,2,1,0:T(8,128)(2,1)} %controls_ref.7), custom_call_target="tpu_custom_call" | custom-call | flops 4194304 | bytes 10485760 | tf_op jit(solution)/shard_map/pallas_call | solution.py:63
  8.5 5.9 %shard_map.73 = f32[64,32,256]{2,1,0:T(8,128)} custom-call(bf16[4,64,128,256]{3,2,1,0:T(8,128)(2,1)} %spread_ref.15, bf16[4,64,128,256]{3,2,1,0:T(8,128)(2,1)} %controls_ref.7), custom_call_target="tpu_custom_call" | custom-call | flops 4194304 | bytes 10485760 | tf_op jit(solution)/shard_map/pallas_call | solution.py:63
  16.6 5.9 %shard_map.79 = f32[64,32,256]{2,1,0:T(8,128)} custom-call(bf16[4,64,128,256]{3,2,1,0:T(8,128)(2,1)} %spread_ref.15, bf16[4,64,128,256]{3,2,1,0:T(8,128)(2,1)} %controls_ref.7), custom_call_target="tpu_custom_call" | custom-call | flops 4194304 | bytes 10485760 | tf_op jit(solution)/shard_map/pallas_call | solution.py:63
  24.4 5.9 %shard_map.77 = f32[64,32,256]{2,1,0:T(8,128)} custom-call(bf16[4,64,128,256]{3,2,1,0:T(8,128)(2,1)} %spread_ref.15, bf16[4,64,128,256]{3,2,1,0:T(8,128)(2,1)} %controls_ref.7), custom_call_target="tpu_custom_call" | custom-call | flops 4194304 | bytes 10485760 | tf_op jit(solution)/shard_map/pallas_call | solution.py:63
  40.0 3.0 collective-permute-start.9
  52.3 3.4 collective-permute-done.1
  55.8 2.1 collective-permute-start.2
  58.0 3.4 collective-permute-done.25
  63.6 2.8 collective-permute-done.17
  68.4 2.7 collective-permute-start.11
  71.6 2.7 collective-permute-start.27
  77.4 4.6 %collective-permute-done.3 = bf16[4,32,256]{2,1,0:T(8,128)(2,1)S(1)} collective-permute-done((bf16[4,32,256]{2,1,0:T(8,128)(2,1)S(1)}, bf16[4,32,256]{2,1,0:T(8,128)(2,1)S(1)}, u32[]{:S(2)}, u32[]{:S(2)}) %collective-permute-start.3) | collective-permute-done | bytes 65568 | tf_op jit(solution)/shard_map/ppermute | solution.py:150
  82.1 3.4 collective-permute-done.19
  85.6 3.0 collective-permute-start.28
  88.6 3.9 %collective-permute-done.20 = bf16[4,32,256]{2,1,0:T(8,128)(2,1)S(1)} collective-permute-done((bf16[4,32,256]{2,1,0:T(8,128)(2,1)S(1)}, bf16[4,32,256]{2,1,0:T(8,128)(2,1)S(1)}, u32[]{:S(2)}, u32[]{:S(2)}) %collective-permute-start.20) | collective-permute-done | bytes 65568 | tf_op jit(solution)/shard_map/ppermute | solution.py:150
  96.1 2.9 collective-permute-done.21
  100.6 2.7 collective-permute-done.29
  103.4 2.3 collective-permute-start.30
  109.0 4.0 %collective-permute-done.30 = bf16[16,32,256]{2,1,0:T(8,128)(2,1)S(1)} collective-permute-done((bf16[16,32,256]{2,1,0:T(8,128)(2,1)S(1)}, bf16[16,32,256]{2,1,0:T(8,128)(2,1)S(1)}, u32[]{:S(2)}, u32[]{:S(2)}) %collective-permute-start.30) | collective-permute-done | bytes 262176 | tf_op jit(solution)/shard_map/ppermute | solution.py:150
  113.9 4.8 %collective-permute-done.14 = bf16[16,32,256]{2,1,0:T(8,128)(2,1)S(1)} collective-permute-done((bf16[16,32,256]{2,1,0:T(8,128)(2,1)S(1)}, bf16[16,32,256]{2,1,0:T(8,128)(2,1)S(1)}, u32[]{:S(2)}, u32[]{:S(2)}) %collective-permute-start.14) | collective-permute-done | bytes 262176 | tf_op jit(solution)/shard_map/ppermute | solution.py:150
  118.8 3.5 %collective-permute-done.6 = bf16[16,32,256]{2,1,0:T(8,128)(2,1)} collective-permute-done((bf16[16,32,256]{2,1,0:T(8,128)(2,1)S(1)}, bf16[16,32,256]{2,1,0:T(8,128)(2,1)}, u32[]{:S(2)}, u32[]{:S(2)}) %collective-permute-start.6) | collective-permute-done | bytes 262176 | tf_op jit(solution)/shard_map/ppermute | solution.py:150
  125.4 18.0 %shard_map.78 = (bf16[4,64,32,128]{3,2,1,0:T(8,128)(2,1)}, bf16[4,64,32,128]{3,2,1,0:T(8,128)(2,1)}) custom-call(bf16[4,64,128,256]{3,2,1,0:T(8,128)(2,1)} %spread_ref.15, bf16[64,32,256]{2,1,0:T(8,128)(2,1)} %maximum_select_fusion.2.weighted_ref, bf16[256,256]{1,0:T(8,128)(2,1)} %maximum_bitcast_fusion.lon_ref, bf16[64,64]{1,0:T(8,128)(2,1)} %vert_ref.7), custom_call_target="tpu_custom_call" | custom-call | flops 1342177280 | bytes 8388608 | tf_op jit(solution)/shard_map/pallas_call | solution.py:111
  144.5 2.4 maximum_select_fusion.3.weighted_ref
  146.9 17.9 %shard_map.80 = (bf16[4,64,32,128]{3,2,1,0:T(8,128)(2,1)}, bf16[4,64,32,128]{3,2,1,0:T(8,128)(2,1)}) custom-call(bf16[4,64,128,256]{3,2,1,0:T(8,128)(2,1)} %spread_ref.15, bf16[64,32,256]{2,1,0:T(8,128)(2,1)} %maximum_select_fusion.3.weighted_ref, bf16[256,256]{1,0:T(8,128)(2,1)} %maximum_bitcast_fusion.lon_ref, bf16[64,64]{1,0:T(8,128)(2,1)} %vert_ref.7), custom_call_target="tpu_custom_call" | custom-call | flops 1342177280 | bytes 8388608 | tf_op jit(solution)/shard_map/pallas_call | solution.py:111
  165.8 2.7 maximum_select_fusion.weighted_ref
  168.4 17.9 %shard_map.74 = (bf16[4,64,32,128]{3,2,1,0:T(8,128)(2,1)}, bf16[4,64,32,128]{3,2,1,0:T(8,128)(2,1)}) custom-call(bf16[4,64,128,256]{3,2,1,0:T(8,128)(2,1)} %spread_ref.15, bf16[64,32,256]{2,1,0:T(8,128)(2,1)} %maximum_select_fusion.weighted_ref, bf16[256,256]{1,0:T(8,128)(2,1)} %maximum_bitcast_fusion.lon_ref, bf16[64,64]{1,0:T(8,128)(2,1)} %vert_ref.7), custom_call_target="tpu_custom_call" | custom-call | flops 1342177280 | bytes 8388608 | tf_op jit(solution)/shard_map/pallas_call | solution.py:111
  187.5 2.4 maximum_select_fusion.1.weighted_ref
  189.9 18.0 %shard_map.76 = (bf16[4,64,32,128]{3,2,1,0:T(8,128)(2,1)}, bf16[4,64,32,128]{3,2,1,0:T(8,128)(2,1)}) custom-call(bf16[4,64,128,256]{3,2,1,0:T(8,128)(2,1)} %spread_ref.15, bf16[64,32,256]{2,1,0:T(8,128)(2,1)} %maximum_select_fusion.1.weighted_ref, bf16[256,256]{1,0:T(8,128)(2,1)} %maximum_bitcast_fusion.lon_ref, bf16[64,64]{1,0:T(8,128)(2,1)} %vert_ref.7), custom_call_target="tpu_custom_call" | custom-call | flops 1342177280 | bytes 8388608 | tf_op jit(solution)/shard_map/pallas_call | solution.py:111
  209.7 27.5 %collective-permute-done.35.refs_7_ = bf16[4,64,32,128]{3,2,1,0:T(8,128)(2,1)} collective-permute-done((bf16[4,64,32,128]{3,2,1,0:T(8,128)(2,1)}, bf16[4,64,32,128]{3,2,1,0:T(8,128)(2,1)}, u32[]{:S(2)}, u32[]{:S(2)}) %collective-permute-start.35) | collective-permute-done | bytes 2097184 | tf_op jit(solution)/shard_map/ppermute | solution.py:182
  237.2 44.9 %collective-permute-done.32.refs_4_ = bf16[4,64,32,128]{3,2,1,0:T(8,128)(2,1)} collective-permute-done((bf16[4,64,32,128]{3,2,1,0:T(8,128)(2,1)}, bf16[4,64,32,128]{3,2,1,0:T(8,128)(2,1)}, u32[]{:S(2)}, u32[]{:S(2)}) %collective-permute-start.32) | collective-permute-done | bytes 2097184 | tf_op jit(solution)/shard_map/ppermute | solution.py:182
  282.1 44.5 %collective-permute-done.33.refs_5_ = bf16[4,64,32,128]{3,2,1,0:T(8,128)(2,1)} collective-permute-done((bf16[4,64,32,128]{3,2,1,0:T(8,128)(2,1)}, bf16[4,64,32,128]{3,2,1,0:T(8,128)(2,1)}, u32[]{:S(2)}, u32[]{:S(2)}) %collective-permute-start.33) | collective-permute-done | bytes 2097184 | tf_op jit(solution)/shard_map/ppermute | solution.py:182
  326.6 26.7 %shard_map.81 = bf16[4,64,128,256]{3,2,1,0:T(8,128)(2,1)} custom-call(bf16[4,64,32,128]{3,2,1,0:T(8,128)(2,1)} %get-tuple-element.13.refs_0_, bf16[4,64,32,128]{3,2,1,0:T(8,128)(2,1)} %get-tuple-element.14.refs_1_, bf16[4,64,32,128]{3,2,1,0:T(8,128)(2,1)} %get-tuple-element.15.refs_2_, bf16[4,64,32,128]{3,2,1,0:T(8,128)(2,1)} %get-tuple-element.16.refs_3_, ...), custom_call_target="tpu_custom_call" | custom-call | tf_op jit(solution)/shard_map/pallas_call | solution.py:39
  (126 shorter events, 51.2 us)
Async XLA Ops:
  8.0 30.3 %collective-permute-start.8 = (bf16[32,32,256]{2,1,0:T(8,128)(2,1)}, bf16[32,32,256]{2,1,0:T(8,128)(2,1)}, u32[]{:S(2)}, u32[]{:S(2)}) collective-permute-start(bf16[32,32,256]{2,1,0:T(8,128)(2,1)} %dynamic-slice_convert_fusion.2), channel_id=1, source_target_pairs={{0,2},{2,0},{4,6},{6,4},{8,10},{10,8},{12,14},{14,12},{16,18},{18,... | collective-permute-start | bytes 1572872 | tf_op jit(solution)/shard_map/ppermute | solution.py:150
  16.5 26.4 %collective-permute-start = (bf16[32,32,256]{2,1,0:T(8,128)(2,1)}, bf16[32,32,256]{2,1,0:T(8,128)(2,1)}, u32[]{:S(2)}, u32[]{:S(2)}) collective-permute-start(bf16[32,32,256]{2,1,0:T(8,128)(2,1)} %dynamic-slice_convert_fusion.3), channel_id=1, source_target_pairs={{0,2},{2,0},{4,6},{6,4},{8,10},{10,8},{12,14},{14,12},{16,18},{18,... | collective-permute-start | bytes 1572872 | tf_op jit(solution)/shard_map/ppermute | solution.py:150
  23.8 20.7 %collective-permute-start.24 = (bf16[32,32,256]{2,1,0:T(8,128)(2,1)S(1)}, bf16[32,32,256]{2,1,0:T(8,128)(2,1)}, u32[]{:S(2)}, u32[]{:S(2)}) collective-permute-start(bf16[32,32,256]{2,1,0:T(8,128)(2,1)S(1)} %dynamic-slice_convert_fusion), channel_id=1, source_target_pairs={{0,2},{2,0},{4,6},{6,4},{8,10},{10,8},{12,14},{14,12},{16,18},{18,... | collective-permute-start | bytes 1572872 | tf_op jit(solution)/shard_map/ppermute | solution.py:150
  31.6 16.1 %collective-permute-start.16 = (bf16[32,32,256]{2,1,0:T(8,128)(2,1)S(1)}, bf16[32,32,256]{2,1,0:T(8,128)(2,1)}, u32[]{:S(2)}, u32[]{:S(2)}) collective-permute-start(bf16[32,32,256]{2,1,0:T(8,128)(2,1)S(1)} %dynamic-slice_convert_fusion.1), channel_id=1, source_target_pairs={{0,2},{2,0},{4,6},{6,4},{8,10},{10,8},{12,14},{14,12},{16,18},{18,... | collective-permute-start | bytes 1572872 | tf_op jit(solution)/shard_map/ppermute | solution.py:150
  40.0 10.1 %collective-permute-start.9 = (bf16[16,32,256]{2,1,0:T(8,128)(2,1)S(1)}, bf16[16,32,256]{2,1,0:T(8,128)(2,1)S(1)}, u32[]{:S(2)}, u32[]{:S(2)}) collective-permute-start(bf16[16,32,256]{2,1,0:T(8,128)(2,1)S(1)} %dynamic-slice_convert_fusion.6), channel_id=1, source_target_pairs={{0,4},{2,6},{4,0},{6,2},{8,12},{10,14},{12,8},{14,10},{16,20},{18,... | collective-permute-start | bytes 786440 | tf_op jit(solution)/shard_map/ppermute | solution.py:150
  44.2 11.5 %collective-permute-start.1 = (bf16[16,32,256]{2,1,0:T(8,128)(2,1)S(1)}, bf16[16,32,256]{2,1,0:T(8,128)(2,1)S(1)}, u32[]{:S(2)}, u32[]{:S(2)}) collective-permute-start(bf16[16,32,256]{2,1,0:T(8,128)(2,1)S(1)} %dynamic-slice_convert_fusion.7), channel_id=1, source_target_pairs={{0,4},{2,6},{4,0},{6,2},{8,12},{10,14},{12,8},{14,10},{16,20},{18,... | collective-permute-start | bytes 786440 | tf_op jit(solution)/shard_map/ppermute | solution.py:150
  45.9 15.4 %collective-permute-start.25 = (bf16[16,32,256]{2,1,0:T(8,128)(2,1)S(1)}, bf16[16,32,256]{2,1,0:T(8,128)(2,1)S(1)}, u32[]{:S(2)}, u32[]{:S(2)}) collective-permute-start(bf16[16,32,256]{2,1,0:T(8,128)(2,1)S(1)} %dynamic-slice_convert_fusion.4), channel_id=1, source_target_pairs={{0,4},{2,6},{4,0},{6,2},{8,12},{10,14},{12,8},{14,10},{16,20},{18,... | collective-permute-start | bytes 786440 | tf_op jit(solution)/shard_map/ppermute | solution.py:150
  49.0 17.4 %collective-permute-start.17 = (bf16[16,32,256]{2,1,0:T(8,128)(2,1)S(1)}, bf16[16,32,256]{2,1,0:T(8,128)(2,1)S(1)}, u32[]{:S(2)}, u32[]{:S(2)}) collective-permute-start(bf16[16,32,256]{2,1,0:T(8,128)(2,1)S(1)} %dynamic-slice_convert_fusion.5), channel_id=1, source_target_pairs={{0,4},{2,6},{4,0},{6,2},{8,12},{10,14},{12,8},{14,10},{16,20},{18,... | collective-permute-start | bytes 786440 | tf_op jit(solution)/shard_map/ppermute | solution.py:150
  50.2 18.1 %collective-permute-start.10 = (bf16[8,32,256]{2,1,0:T(8,128)(2,1)S(1)}, bf16[8,32,256]{2,1,0:T(8,128)(2,1)S(1)}, u32[]{:S(2)}, u32[]{:S(2)}) collective-permute-start(bf16[8,32,256]{2,1,0:T(8,128)(2,1)S(1)} %dynamic-slice_convert_fusion.10), channel_id=1, source_target_pairs={{0,8},{2,10},{4,12},{6,14},{8,0},{10,2},{12,4},{14,6},{16,24},{18,... | collective-permute-start | bytes 393224 | tf_op jit(solution)/shard_map/ppermute | solution.py:150
  55.8 15.2 %collective-permute-start.2 = (bf16[8,32,256]{2,1,0:T(8,128)(2,1)S(1)}, bf16[8,32,256]{2,1,0:T(8,128)(2,1)S(1)}, u32[]{:S(2)}, u32[]{:S(2)}) collective-permute-start(bf16[8,32,256]{2,1,0:T(8,128)(2,1)S(1)} %dynamic-slice_convert_fusion.11), channel_id=1, source_target_pairs={{0,8},{2,10},{4,12},{6,14},{8,0},{10,2},{12,4},{14,6},{16,24},{18,... | collective-permute-start | bytes 393224 | tf_op jit(solution)/shard_map/ppermute | solution.py:150
  61.4 10.1 %collective-permute-start.26 = (bf16[8,32,256]{2,1,0:T(8,128)(2,1)S(1)}, bf16[8,32,256]{2,1,0:T(8,128)(2,1)S(1)}, u32[]{:S(2)}, u32[]{:S(2)}) collective-permute-start(bf16[8,32,256]{2,1,0:T(8,128)(2,1)S(1)} %dynamic-slice_convert_fusion.8), channel_id=1, source_target_pairs={{0,8},{2,10},{4,12},{6,14},{8,0},{10,2},{12,4},{14,6},{16,24},{18,... | collective-permute-start | bytes 393224 | tf_op jit(solution)/shard_map/ppermute | solution.py:150
  66.5 7.7 %collective-permute-start.18 = (bf16[8,32,256]{2,1,0:T(8,128)(2,1)S(1)}, bf16[8,32,256]{2,1,0:T(8,128)(2,1)S(1)}, u32[]{:S(2)}, u32[]{:S(2)}) collective-permute-start(bf16[8,32,256]{2,1,0:T(8,128)(2,1)S(1)} %dynamic-slice_convert_fusion.9), channel_id=1, source_target_pairs={{0,8},{2,10},{4,12},{6,14},{8,0},{10,2},{12,4},{14,6},{16,24},{18,... | collective-permute-start | bytes 393224 | tf_op jit(solution)/shard_map/ppermute | solution.py:150
  71.1 10.8 %collective-permute-start.3 = (bf16[4,32,256]{2,1,0:T(8,128)(2,1)S(1)}, bf16[4,32,256]{2,1,0:T(8,128)(2,1)S(1)}, u32[]{:S(2)}, u32[]{:S(2)}) collective-permute-start(bf16[4,32,256]{2,1,0:T(8,128)(2,1)S(1)} %dynamic-slice_convert_fusion.15), channel_id=1, source_target_pairs={{0,16},{2,18},{4,20},{6,22},{8,24},{10,26},{12,28},{14,30},{16,0},... | collective-permute-start | bytes 196616 | tf_op jit(solution)/shard_map/ppermute | solution.py:150
  71.6 14.0 %collective-permute-start.27 = (bf16[4,32,256]{2,1,0:T(8,128)(2,1)S(1)}, bf16[4,32,256]{2,1,0:T(8,128)(2,1)S(1)}, u32[]{:S(2)}, u32[]{:S(2)}) collective-permute-start(bf16[4,32,256]{2,1,0:T(8,128)(2,1)S(1)} %dynamic-slice_convert_fusion.12), channel_id=1, source_target_pairs={{0,16},{2,18},{4,20},{6,22},{8,24},{10,26},{12,28},{14,30},{16,0},... | collective-permute-start | bytes 196616 | tf_op jit(solution)/shard_map/ppermute | solution.py:150
  74.3 11.2 %collective-permute-start.19 = (bf16[4,32,256]{2,1,0:T(8,128)(2,1)S(1)}, bf16[4,32,256]{2,1,0:T(8,128)(2,1)S(1)}, u32[]{:S(2)}, u32[]{:S(2)}) collective-permute-start(bf16[4,32,256]{2,1,0:T(8,128)(2,1)S(1)} %dynamic-slice_convert_fusion.13), channel_id=1, source_target_pairs={{0,16},{2,18},{4,20},{6,22},{8,24},{10,26},{12,28},{14,30},{16,0},... | collective-permute-start | bytes 196616 | tf_op jit(solution)/shard_map/ppermute | solution.py:150
  75.7 16.9 %collective-permute-start.12 = (bf16[4,32,256]{2,1,0:T(8,128)(2,1)S(1)}, bf16[4,32,256]{2,1,0:T(8,128)(2,1)S(1)}, u32[]{:S(2)}, u32[]{:S(2)}) collective-permute-start(bf16[4,32,256]{2,1,0:T(8,128)(2,1)S(1)} %fusion.6), channel_id=1, source_target_pairs={{0,16},{2,18},{4,20},{6,22},{8,24},{10,26},{12,28},{14,30},{16,0},... | collective-permute-start | bytes 196616 | tf_op jit(solution)/shard_map/ppermute | solution.py:150
  82.0 18.6 %collective-permute-start.4 = (bf16[4,32,256]{2,1,0:T(8,128)(2,1)S(1)}, bf16[4,32,256]{2,1,0:T(8,128)(2,1)S(1)}, u32[]{:S(2)}, u32[]{:S(2)}) collective-permute-start(bf16[4,32,256]{2,1,0:T(8,128)(2,1)S(1)} %fusion.7), channel_id=1, source_target_pairs={{0,16},{2,18},{4,20},{6,22},{8,24},{10,26},{12,28},{14,30},{16,0},... | collective-permute-start | bytes 196616 | tf_op jit(solution)/shard_map/ppermute | solution.py:150
  85.6 9.0 %collective-permute-start.28 = (bf16[4,32,256]{2,1,0:T(8,128)(2,1)S(1)}, bf16[4,32,256]{2,1,0:T(8,128)(2,1)S(1)}, u32[]{:S(2)}, u32[]{:S(2)}) collective-permute-start(bf16[4,32,256]{2,1,0:T(8,128)(2,1)S(1)} %fusion.4), channel_id=1, source_target_pairs={{0,16},{2,18},{4,20},{6,22},{8,24},{10,26},{12,28},{14,30},{16,0},... | collective-permute-start | bytes 196616 | tf_op jit(solution)/shard_map/ppermute | solution.py:150
  92.6 13.1 %collective-permute-start.13 = (bf16[8,32,256]{2,1,0:T(8,128)(2,1)S(1)}, bf16[8,32,256]{2,1,0:T(8,128)(2,1)S(1)}, u32[]{:S(2)}, u32[]{:S(2)}) collective-permute-start(bf16[8,32,256]{2,1,0:T(8,128)(2,1)S(1)} %maximum_select_fusion.13), channel_id=1, source_target_pairs={{0,8},{2,10},{4,12},{6,14},{8,0},{10,2},{12,4},{14,6},{16,24},{18,... | collective-permute-start | bytes 393224 | tf_op jit(solution)/shard_map/ppermute | solution.py:150
  94.7 8.7 %collective-permute-start.29 = (bf16[8,32,256]{2,1,0:T(8,128)(2,1)S(1)}, bf16[8,32,256]{2,1,0:T(8,128)(2,1)S(1)}, u32[]{:S(2)}, u32[]{:S(2)}) collective-permute-start(bf16[8,32,256]{2,1,0:T(8,128)(2,1)S(1)} %maximum_select_fusion.15), channel_id=1, source_target_pairs={{0,8},{2,10},{4,12},{6,14},{8,0},{10,2},{12,4},{14,6},{16,24},{18,... | collective-permute-start | bytes 393224 | tf_op jit(solution)/shard_map/ppermute | solution.py:150
  99.0 8.5 %collective-permute-start.22 = (bf16[16,32,256]{2,1,0:T(8,128)(2,1)S(1)}, bf16[16,32,256]{2,1,0:T(8,128)(2,1)S(1)}, u32[]{:S(2)}, u32[]{:S(2)}) collective-permute-start(bf16[16,32,256]{2,1,0:T(8,128)(2,1)S(1)} %maximum_select_fusion.10), channel_id=1, source_target_pairs={{0,4},{2,6},{4,0},{6,2},{8,12},{10,14},{12,8},{14,10},{16,20},{18,... | collective-permute-start | bytes 786440 | tf_op jit(solution)/shard_map/ppermute | solution.py:150
  103.4 9.6 %collective-permute-start.30 = (bf16[16,32,256]{2,1,0:T(8,128)(2,1)S(1)}, bf16[16,32,256]{2,1,0:T(8,128)(2,1)S(1)}, u32[]{:S(2)}, u32[]{:S(2)}) collective-permute-start(bf16[16,32,256]{2,1,0:T(8,128)(2,1)S(1)} %maximum_select_fusion.11), channel_id=1, source_target_pairs={{0,4},{2,6},{4,0},{6,2},{8,12},{10,14},{12,8},{14,10},{16,20},{18,... | collective-permute-start | bytes 786440 | tf_op jit(solution)/shard_map/ppermute | solution.py:150
  105.7 12.9 %collective-permute-start.14 = (bf16[16,32,256]{2,1,0:T(8,128)(2,1)S(1)}, bf16[16,32,256]{2,1,0:T(8,128)(2,1)S(1)}, u32[]{:S(2)}, u32[]{:S(2)}) collective-permute-start(bf16[16,32,256]{2,1,0:T(8,128)(2,1)S(1)} %maximum_select_fusion.9), channel_id=1, source_target_pairs={{0,4},{2,6},{4,0},{6,2},{8,12},{10,14},{12,8},{14,10},{16,20},{18,... | collective-permute-start | bytes 786440 | tf_op jit(solution)/shard_map/ppermute | solution.py:150
  107.5 16.8 %collective-permute-start.23 = (bf16[32,32,256]{2,1,0:T(8,128)(2,1)S(1)}, bf16[32,32,256]{2,1,0:T(8,128)(2,1)S(1)}, u32[]{:S(2)}, u32[]{:S(2)}) collective-permute-start(bf16[32,32,256]{2,1,0:T(8,128)(2,1)S(1)} %maximum_select_fusion.6), channel_id=1, source_target_pairs={{0,2},{2,0},{4,6},{6,4},{8,10},{10,8},{12,14},{14,12},{16,18},{18,... | collective-permute-start | bytes 1572872 | tf_op jit(solution)/shard_map/ppermute | solution.py:150
  107.6 14.7 %collective-permute-start.6 = (bf16[16,32,256]{2,1,0:T(8,128)(2,1)S(1)}, bf16[16,32,256]{2,1,0:T(8,128)(2,1)}, u32[]{:S(2)}, u32[]{:S(2)}) collective-permute-start(bf16[16,32,256]{2,1,0:T(8,128)(2,1)S(1)} %maximum_select_fusion.8), channel_id=1, source_target_pairs={{0,4},{2,6},{4,0},{6,2},{8,12},{10,14},{12,8},{14,10},{16,20},{18,... | collective-permute-start | bytes 786440 | tf_op jit(solution)/shard_map/ppermute | solution.py:150
  113.1 31.4 %collective-permute-start.31 = (bf16[32,32,256]{2,1,0:T(8,128)(2,1)S(1)}, bf16[32,32,256]{2,1,0:T(8,128)(2,1)}, u32[]{:S(2)}, u32[]{:S(2)}) collective-permute-start(bf16[32,32,256]{2,1,0:T(8,128)(2,1)S(1)} %maximum_select_fusion.7), channel_id=1, source_target_pairs={{0,2},{2,0},{4,6},{6,4},{8,10},{10,8},{12,14},{14,12},{16,18},{18,... | collective-permute-start | bytes 1572872 | tf_op jit(solution)/shard_map/ppermute | solution.py:150
  118.7 68.7 %collective-permute-start.15 = (bf16[32,32,256]{2,1,0:T(8,128)(2,1)S(1)}, bf16[32,32,256]{2,1,0:T(8,128)(2,1)}, u32[]{:S(2)}, u32[]{:S(2)}) collective-permute-start(bf16[32,32,256]{2,1,0:T(8,128)(2,1)S(1)} %maximum_select_fusion.5), channel_id=1, source_target_pairs={{0,2},{2,0},{4,6},{6,4},{8,10},{10,8},{12,14},{14,12},{16,18},{18,... | collective-permute-start | bytes 1572872 | tf_op jit(solution)/shard_map/ppermute | solution.py:150
  124.3 41.5 %collective-permute-start.7 = (bf16[32,32,256]{2,1,0:T(8,128)(2,1)}, bf16[32,32,256]{2,1,0:T(8,128)(2,1)}, u32[]{:S(2)}, u32[]{:S(2)}) collective-permute-start(bf16[32,32,256]{2,1,0:T(8,128)(2,1)} %maximum_select_fusion.4), channel_id=1, source_target_pairs={{0,2},{2,0},{4,6},{6,4},{8,10},{10,8},{12,14},{14,12},{16,18},{18,... | collective-permute-start | bytes 1572872 | tf_op jit(solution)/shard_map/ppermute | solution.py:150
  143.4 66.2 %collective-permute-start.34 = (bf16[4,64,32,128]{3,2,1,0:T(8,128)(2,1)}, bf16[4,64,32,128]{3,2,1,0:T(8,128)(2,1)S(1)}, u32[]{:S(2)}, u32[]{:S(2)}) collective-permute-start(bf16[4,64,32,128]{3,2,1,0:T(8,128)(2,1)} %get-tuple-element.19), channel_id=1, source_target_pairs={{0,1},{1,0},{2,3},{3,2},{4,5},{5,4},{6,7},{7,6},{8,9},{9,8},{10,11... | collective-permute-start | bytes 6291464 | tf_op jit(solution)/shard_map/ppermute | solution.py:182
  164.8 72.4 %collective-permute-start.35 = (bf16[4,64,32,128]{3,2,1,0:T(8,128)(2,1)}, bf16[4,64,32,128]{3,2,1,0:T(8,128)(2,1)}, u32[]{:S(2)}, u32[]{:S(2)}) collective-permute-start(bf16[4,64,32,128]{3,2,1,0:T(8,128)(2,1)} %get-tuple-element.20), channel_id=1, source_target_pairs={{0,1},{1,0},{2,3},{3,2},{4,5},{5,4},{6,7},{7,6},{8,9},{9,8},{10,11... | collective-permute-start | bytes 6291464 | tf_op jit(solution)/shard_map/ppermute | solution.py:182
  186.4 95.8 %collective-permute-start.32 = (bf16[4,64,32,128]{3,2,1,0:T(8,128)(2,1)}, bf16[4,64,32,128]{3,2,1,0:T(8,128)(2,1)}, u32[]{:S(2)}, u32[]{:S(2)}) collective-permute-start(bf16[4,64,32,128]{3,2,1,0:T(8,128)(2,1)} %get-tuple-element.17), channel_id=1, source_target_pairs={{0,1},{1,0},{2,3},{3,2},{4,5},{5,4},{6,7},{7,6},{8,9},{9,8},{10,11... | collective-permute-start | bytes 6291464 | tf_op jit(solution)/shard_map/ppermute | solution.py:182
  207.8 118.8 %collective-permute-start.33 = (bf16[4,64,32,128]{3,2,1,0:T(8,128)(2,1)}, bf16[4,64,32,128]{3,2,1,0:T(8,128)(2,1)}, u32[]{:S(2)}, u32[]{:S(2)}) collective-permute-start(bf16[4,64,32,128]{3,2,1,0:T(8,128)(2,1)} %get-tuple-element.18), channel_id=1, source_target_pairs={{0,1},{1,0},{2,3},{3,2},{4,5},{5,4},{6,7},{7,6},{8,9},{9,8},{10,11... | collective-permute-start | bytes 6291464 | tf_op jit(solution)/shard_map/ppermute | solution.py:182
  (12 other events, 248.9 us)
